TPU v7x, 256 devices: a whole 4x4x8 slice. The times are simulated.
256 devices in a mesh: expert: 64 (over z, x, core), tensor: 4 (over y).
Axes of the slice: x: 4, y: 4, z: 8, core: 2. Of those that a mesh axis runs over, the one named last changes fastest.
Arguments:
- tokens: bfloat16 [2048, 4096], P('expert', 'tensor'), may hold values from -6 to 6
- cotangent: bfloat16 [2048, 4096], P('expert', 'tensor'), may hold values from -6 to 6
- routing: int32 [2048, 8], P('expert'), may hold values from 0 to 63, as said below
- gates: float32 [2048, 8], P('expert'), may hold values from 0.1 to 0.4
- w_in: bfloat16 [64, 4096, 1536], P('expert', None, 'tensor'), may hold values from -0.09375 to 0.09375
- w_out: bfloat16 [64, 1536, 4096], P('expert', 'tensor'), may hold values from -0.15625 to 0.15625
Outputs:
- mixed: bfloat16 [2048, 4096], P('expert', 'tensor')
- d_tokens: bfloat16 [2048, 4096], P('expert', 'tensor')
- d_w_in: bfloat16 [64, 4096, 1536], P('expert', None, 'tensor')
- d_w_out: bfloat16 [64, 1536, 4096], P('expert', 'tensor')
Inputs may be any that keep to these rules, and one draw needn't show every extreme that they name: `routing`: each row names 8 different experts. In each aligned block of 32 rows (the tokens of one index of the expert axis) no expert is named by more than 8 rows, and one expert is named by exactly 8 rows of every block.
All inputs are finite; a program needn't handle non-finite values.
Results may differ from a plain program's by a relative error of at most 0.0058.
Values may be sent and summed in bfloat16 or wider, within the bound.
A program may use at most 128 MiB of HBM per device.

v0:
```python
import jax
import jax.numpy as jnp
from jax import lax
from jax.sharding import PartitionSpec as P


def shards(tokens, cotangent, routing, gates, w_in, w_out):
    devices = lax.axis_size("expert")
    local_experts = w_in.shape[0]
    experts = devices * local_experts
    tok_rows = routing.shape[0]
    capacity = tok_rows // 4
    buffer_rows = experts * capacity
    highest = lax.Precision.HIGHEST
    matches = (routing[:, :, None] == jnp.arange(experts, dtype=jnp.int32)[None, None, :]).astype(
        jnp.int32
    )
    per_token = jnp.sum(matches, axis=1)
    earlier = jnp.cumsum(per_token, axis=0) - per_token
    destination = routing * capacity + jnp.take_along_axis(earlier, routing, axis=1)
    placed = (
        destination[:, :, None] == jnp.arange(buffer_rows, dtype=jnp.int32)[None, None, :]
    ).astype(jnp.float32)
    membership = jnp.sum(placed, axis=1)
    weighting = jnp.sum(placed * gates[:, :, None], axis=1)
    whole_tokens, whole_cot = (
        lax.all_gather(tokens, "tensor", axis=1, tiled=True),
        lax.all_gather(cotangent, "tensor", axis=1, tiled=True),
    )
    width = whole_tokens.shape[1]
    rows = jnp.einsum(
        "tr,td->rd",
        membership.astype(jnp.bfloat16),
        whole_tokens,
        preferred_element_type=jnp.float32,
    ).astype(jnp.bfloat16)
    scaled = jnp.einsum(
        "tr,td->rd", weighting, whole_cot.astype(jnp.float32), precision=highest
    ).astype(jnp.bfloat16)
    send_rows = rows.reshape(devices, local_experts, capacity, width)
    send_scaled = scaled.reshape(devices, local_experts, capacity, width)
    expert_rows, expert_scaled = (
        lax.all_to_all(send_rows, "expert", split_axis=0, concat_axis=0, tiled=True),
        lax.all_to_all(send_scaled, "expert", split_axis=0, concat_axis=0, tiled=True),
    )
    preact = jnp.einsum("nesd,edh->nesh", expert_rows, w_in, preferred_element_type=jnp.float32)
    sigmoid_val = jax.nn.sigmoid(preact)
    hidden = (preact * sigmoid_val).astype(jnp.bfloat16)
    out_part = jnp.einsum("nesh,ehd->nesd", hidden, w_out, preferred_element_type=jnp.float32)
    grad_hidden = jnp.einsum(
        "nesd,ehd->nesh", expert_scaled, w_out, preferred_element_type=jnp.float32
    )
    grad_preact = (grad_hidden * sigmoid_val * (1.0 + preact * (1.0 - sigmoid_val))).astype(
        jnp.bfloat16
    )
    d_w_out = jnp.einsum(
        "nesh,nesd->ehd", hidden, expert_scaled, preferred_element_type=jnp.float32
    ).astype(jnp.bfloat16)
    d_w_in = jnp.einsum(
        "nesd,nesh->edh", expert_rows, grad_preact, preferred_element_type=jnp.float32
    ).astype(jnp.bfloat16)
    grad_part = jnp.einsum("nesh,edh->nesd", grad_preact, w_in, preferred_element_type=jnp.float32)
    out_sums, grad_sums = (
        lax.psum_scatter(out_part, "tensor", scatter_dimension=3, tiled=True),
        lax.psum_scatter(grad_part, "tensor", scatter_dimension=3, tiled=True),
    )
    back_out, back_grad = (
        lax.all_to_all(out_sums, "expert", split_axis=0, concat_axis=0, tiled=True),
        lax.all_to_all(grad_sums, "expert", split_axis=0, concat_axis=0, tiled=True),
    )
    width_q = back_out.shape[3]
    mixed = jnp.einsum(
        "tr,rd->td", weighting, back_out.reshape(buffer_rows, width_q), precision=highest
    ).astype(jnp.bfloat16)
    d_tokens = jnp.einsum(
        "tr,rd->td", membership, back_grad.reshape(buffer_rows, width_q), precision=highest
    ).astype(jnp.bfloat16)
    return (mixed, d_tokens, d_w_in, d_w_out)


def solution(mesh):
    placed = (
        P("expert", "tensor"),
        P("expert", "tensor"),
        P("expert", None),
        P("expert", None),
        P("expert", None, "tensor"),
        P("expert", "tensor", None),
    )
    return jax.shard_map(
        shards,
        mesh=mesh,
        in_specs=placed,
        out_specs=(
            P("expert", "tensor"),
            P("expert", "tensor"),
            P("expert", None, "tensor"),
            P("expert", "tensor", None),
        ),
        check_vma=False,
    )
```

profile of v0, /device:TPU:2, one launch (start us, length us, event | category | flops | bytes accessed | tf_op | source)
XLA Modules:
  0.0 423.1 jit_solution(5423124009950122582)
XLA Ops:
  7.2 0.0 copy-start
  7.2 0.0 reduce-scatter.3.cloned.1.call-start
  7.2 0.8 bitcast_or_fusion
  8.1 0.8 copy.47
  8.9 0.1 copy.48
  9.0 0.1 reshape.75
  9.1 0.8 copy.51
  9.8 0.1 convert_reduce_fusion.1
  9.9 0.1 reduce_window_sum.11
  10.0 0.0 copy-start.10
  10.0 0.0 copy-start.8
  10.0 1.9 gather_fusion
  12.0 0.1 reshape.78
  12.1 0.1 copy.49
  12.1 0.0 copy-done.10
  12.1 0.1 copy.50
  12.2 0.0 copy-done.8
  12.2 12.8 %all_gather.6 = bf16[32,4096]{1,0:T(8,128)(2,1)S(1)} all-gather(bf16[32,1024]{1,0:T(8,128)(2,1)S(1)} %copy-done.8), channel_id=1, replica_groups=mesh['expert'=64,'tensor'=4] {'tensor'}, dimensions={1}, use_global_device_ids=true | all-gather | bytes 327680 | tf_op jit(solution)/shard_map/all_gather | solution.py:27
  25.0 0.4 convert_reduce_fusion
  25.4 1.3 fusion
  26.7 0.0 copy-start.3
  26.7 108.3 %all_to_all.20 = bf16[64,1,8,4096]{3,2,1,0:T(8,128)(2,1)S(1)} all-to-all(bf16[64,1,8,4096]{3,2,1,0:T(8,128)(2,1)S(1)} %fusion), channel_id=1, replica_groups=mesh['expert'=64,'tensor'=4] {'expert'}, dimensions={0} | all-to-all | bytes 8388608 | tf_op jit(solution)/shard_map/all_to_all | solution.py:43
  135.0 0.0 copy-done.3
  135.0 0.0 copy-start.1
  135.0 2.3 fusion.18
  137.3 0.0 copy-done.1
  137.3 0.0 copy-start.5
  137.3 0.9 copy-done.5
  138.2 0.0 copy-done
  138.2 5.6 %convolution_bitcast_fusion.1 = f32[64,1,8,4096]{3,2,0,1:T(8,128)} fusion(bf16[1,384,4096]{2,1,0:T(8,128)(2,1)S(1)} %copy-done, f32[64,1,8,384]{3,2,0,1:T(8,128)S(1)} %fusion.18), kind=kOutput, calls=%fused_computation.2 | convolution fusion | flops 1611595776 | bytes 12320768 | tf_op jit(solution)/shard_map/nesh,ehd->nesd/dot_general | solution.py:49
  143.8 0.0 copy-start.9
  143.8 0.0 reduce-scatter.3.cloned.1.call-update
  143.8 0.0 reduce-scatter.5.cloned.1.call-start
  143.9 0.8 copy-done.9
  144.6 13.1 %all_gather.7 = bf16[32,4096]{1,0:T(8,128)(2,1)S(1)} all-gather(bf16[32,1024]{1,0:T(8,128)(2,1)S(1)} %copy-done.9), channel_id=1, replica_groups=mesh['expert'=64,'tensor'=4] {'tensor'}, dimensions={1}, use_global_device_ids=true | all-gather | bytes 327680 | tf_op jit(solution)/shard_map/all_gather | solution.py:28
  157.7 3.7 fusion.1
  161.5 0.0 copy-start.6
  161.5 101.6 %all_to_all.21 = bf16[64,1,8,4096]{3,2,1,0:T(8,128)(2,1)S(1)} all-to-all(bf16[64,1,8,4096]{3,2,1,0:T(8,128)(2,1)S(1)} %fusion.1), channel_id=1, replica_groups=mesh['expert'=64,'tensor'=4] {'expert'}, dimensions={0} | all-to-all | bytes 8388608 | tf_op jit(solution)/shard_map/all_to_all | solution.py:44
  263.1 0.0 copy-done.6
  263.1 0.0 copy-start.2
  263.1 0.0 copy-start.4
  263.1 2.4 fusion.43
  265.5 0.0 copy-done.2
  265.5 0.0 copy-start.7
  265.5 0.7 copy-done.7
  266.3 0.2 copy-done.4
  266.5 5.6 %convolution_bitcast_fusion = f32[64,1,8,4096]{3,2,0,1:T(8,128)} fusion(bf16[64,8,384]{2,1,0:T(8,128)(2,1)S(1)} %fusion.43, bf16[1,4096,384]{2,1,0:T(8,128)(2,1)S(1)} %copy-done.4), kind=kOutput, calls=%fused_computation.1 | convolution fusion | flops 1610612736 | bytes 11927552 | tf_op jit(solution)/shard_map/nesh,edh->nesd/dot_general | solution.py:62
  272.1 0.0 reduce-scatter.5.cloned.1.call-update
  272.1 0.0 reduce-scatter.3.cloned.1.call-done
  272.1 5.6 %all-to-all-start.1 = ((f32[64,1,8,1024]{3,2,1,0:T(8,128)}), f32[64,1,8,1024]{3,2,1,0:T(8,128)}, u32[]{:S(2)}, u32[]{:S(2)}) async-start(f32[64,1,8,1024]{3,2,1,0:T(8,128)} %bitcast.128), calls=%async_computation.2 | async-start | bytes 4194304 | tf_op jit(solution)/shard_map/all_to_all | solution.py:68
  277.8 6.8 %fusion.3 = bf16[1,384,4096]{2,1,0:T(8,128)(2,1)} fusion(bf16[64,1,8,4096]{3,2,1,0:T(8,128)(2,1)} %copy-done.2, f32[64,1,8,384]{3,2,0,1:T(8,128)} %copy-done.5), kind=kOutput, calls=%fused_computation.10 | convolution fusion | flops 1613168640 | bytes 8126464 | tf_op jit(solution)/shard_map/nesh,nesd->ehd/dot_general | solution.py:56
  284.5 66.3 %reduce-scatter.5.cloned.1.call-done = f32[64,1,8,1024]{3,2,0,1:T(8,128)} async-done(((f32[64,1,8,4096]{3,2,0,1:T(8,128)}), f32[64,1,8,1024]{3,2,0,1:T(8,128)}) %reduce-scatter.5.cloned.1.call-update) | async-done | bytes 2097168 | tf_op jit(solution)/shard_map/reduce_scatter | solution.py:65
  350.9 0.0 all-to-all-done.1
  350.9 10.7 %all-to-all-start.3 = ((f32[64,1,8,1024]{3,2,1,0:T(8,128)}), f32[64,1,8,1024]{3,2,1,0:T(8,128)}, u32[]{:S(2)}, u32[]{:S(2)}) async-start(f32[64,1,8,1024]{3,2,1,0:T(8,128)} %bitcast.129), calls=%async_computation.5 | async-start | bytes 4194304 | tf_op jit(solution)/shard_map/all_to_all | solution.py:69
  361.6 6.3 %fusion.2 = bf16[1,4096,384]{2,1,0:T(8,128)(2,1)} fusion(bf16[64,8,384]{2,1,0:T(8,128)(2,1)} %copy-done.7, bf16[64,1,8,4096]{3,2,1,0:T(8,128)(2,1)} %copy-done.1), kind=kOutput, calls=%fused_computation.9 | convolution fusion | flops 1612185600 | bytes 7733248 | tf_op jit(solution)/shard_map/nesd,nesh->edh/dot_general | solution.py:59
  367.9 3.5 fusion.48
  371.4 41.3 %all-to-all-done.3 = f32[64,1,8,1024]{3,2,1,0:T(8,128)} async-done(((f32[64,1,8,1024]{3,2,1,0:T(8,128)}), f32[64,1,8,1024]{3,2,1,0:T(8,128)}, u32[]{:S(2)}, u32[]{:S(2)}) %all-to-all-start.3) | async-done | bytes 2097184 | tf_op jit(solution)/shard_map/all_to_all | solution.py:69
  412.8 3.5 fusion.51
  (2 shorter events, 0.0 us)
Async XLA Ops:
  7.2 131.1 %copy-start = (bf16[1,384,4096]{2,1,0:T(8,128)(2,1)S(1)}, bf16[1,384,4096]{2,1,0:T(8,128)(2,1)}, u32[]{:S(2)}) copy-start(bf16[1,384,4096]{2,1,0:T(8,128)(2,1)} %param.11) | copy-start | bytes 9437188
  7.2 264.9 %reduce-scatter.3.cloned.1.call-start = ((), (), s32[]{:S(2)}) async-start(), calls=%async_computation.6 | async-start | bytes 10485760 | tf_op jit(solution)/shard_map/reduce_scatter | solution.py:64
  10.0 2.1 copy-start.10
  10.0 2.2 copy-start.8
  26.7 108.3 %copy-start.3 = (bf16[1,4096,384]{2,1,0:T(8,128)(2,1)S(1)}, bf16[1,4096,384]{2,1,0:T(8,128)(2,1)}, u32[]{:S(2)}) copy-start(bf16[1,4096,384]{2,1,0:T(8,128)(2,1)} %param.10) | copy-start | bytes 9437188
  135.0 2.3 copy-start.1
  137.3 0.9 copy-start.5
  143.8 0.8 copy-start.9
  143.8 207.1 %reduce-scatter.5.cloned.1.call-start = ((), (), s32[]{:S(2)}) async-start(), calls=%async_computation.7 | async-start | bytes 10485760 | tf_op jit(solution)/shard_map/reduce_scatter | solution.py:65
  161.5 101.6 %copy-start.6 = (f32[64,1,8,384]{3,2,0,1:T(8,128)S(1)}, f32[64,1,8,384]{3,2,0,1:T(8,128)}, u32[]{:S(2)}) copy-start(f32[64,1,8,384]{3,2,0,1:T(8,128)} %copy-done.5) | copy-start | bytes 2359300
  263.1 2.5 copy-start.2
  263.1 3.4 copy-start.4
  265.5 0.7 copy-start.7
  272.1 78.7 %all-to-all-start.1 = ((f32[64,1,8,1024]{3,2,1,0:T(8,128)}), f32[64,1,8,1024]{3,2,1,0:T(8,128)}, u32[]{:S(2)}, u32[]{:S(2)}) async-start(f32[64,1,8,1024]{3,2,1,0:T(8,128)} %bitcast.128), calls=%async_computation.2 | async-start | bytes 4194304 | tf_op jit(solution)/shard_map/all_to_all | solution.py:68
  350.9 61.9 %all-to-all-start.3 = ((f32[64,1,8,1024]{3,2,1,0:T(8,128)}), f32[64,1,8,1024]{3,2,1,0:T(8,128)}, u32[]{:S(2)}, u32[]{:S(2)}) async-start(f32[64,1,8,1024]{3,2,1,0:T(8,128)} %bitcast.129), calls=%async_computation.5 | async-start | bytes 4194304 | tf_op jit(solution)/shard_map/all_to_all | solution.py:69
Sparse Core Ops, SparseCore 0:
  143.9 79.4 reduce-scatter.2
  272.2 78.6 reduce-scatter.4
where the time goes:
time: 424 us; the launch traced here: 423 us
  blocking collectives  236 us (56%)
  waiting for transfers between devices  108 us (25%)
  matrix products  41 us (10%)
  starting transfers between devices  16.4 us (4%)
  between operations  14.2 us (3%)
  local copies, waits for them, and re-layouts  6.55 us (2%)
    all_to_all x1, blocking collectives, shards(): lax.all_to_all(send_rows, 'expert', split_axis=0, concat_axis=0, tiled=True)  108 us
    all_to_all x1, blocking collectives, shards(): lax.all_to_all(send_scaled, 'expert', split_axis=0, concat_axis=0, tiled=...  102 us
    reduce_scatter x1, waiting for transfers between devices, shards(): lax.psum_scatter(grad_part, 'tensor', scatter_dimension=3, tiled=True)  66.3 us
    all_to_all x1, waiting for transfers between devices, shards(): lax.all_to_all(grad_sums, 'expert', split_axis=0, concat_axis=0, tiled=True)  41.3 us
    all_gather x1, blocking collectives, shards(): lax.all_gather(cotangent, 'tensor', axis=1, tiled=True)  13.1 us
    all_gather x1, blocking collectives, shards(): lax.all_gather(tokens, 'tensor', axis=1, tiled=True)  12.8 us
    all_to_all x1, starting transfers between devices, shards(): lax.all_to_all(grad_sums, 'expert', split_axis=0, concat_axis=0, tiled=True)  10.7 us
  transfers between devices with their start and end apart: 4, of which 2 were waited for; matrix products, arithmetic and copies ran while one was open for 7% of the time, Pallas kernels for 0%

commit v1 on v0

--- a/solution.py
+++ b/solution.py
@@ -2,6 +2,13 @@
 import jax.numpy as jnp
 from jax import lax
 from jax.sharding import PartitionSpec as P
+
+
+def exchange_gather(x, name, along):
+    size = lax.axis_size(name)
+    blocks = jnp.stack([x for _ in range(size)])
+    blocks = lax.all_to_all(blocks, name, split_axis=0, concat_axis=0)
+    return jnp.concatenate(blocks, axis=along)
 
 
 def shards(tokens, cotangent, routing, gates, w_in, w_out):
@@ -24,7 +31,7 @@
     membership = jnp.sum(placed, axis=1)
     weighting = jnp.sum(placed * gates[:, :, None], axis=1)
     whole_tokens, whole_cot = (
-        lax.all_gather(tokens, "tensor", axis=1, tiled=True),
+        exchange_gather(tokens, "tensor", 1),
         lax.all_gather(cotangent, "tensor", axis=1, tiled=True),
     )
     width = whole_tokens.shape[1]

time: 424 us -> 418 us (0.986)
  blocking collectives: 236 us -> 223 us
  starting transfers between devices: 16.4 us -> 20.9 us
    all_gather x1 -> x0, blocking collectives: 12.8 us -> none  [shards(): lax.all_gather(tokens, 'tensor', axis=1, tiled=True)]
    all_to_all x0 -> x1, starting transfers between devices: none -> 4.46 us  [exchange_gather(): blocks = lax.all_to_all(blocks, name, split_axis=0, concat_axis=0)]
  transfers between devices with their start and end apart: 4 -> 5, of which waited for: 2 -> 3; matrix products, arithmetic and copies ran while one was open for 7% -> 8% of each run, Pallas kernels for 0% -> 0%
where the time goes in v1:
time: 418 us; the launch traced here: 417 us
  blocking collectives  223 us (53%)
  waiting for transfers between devices  109 us (26%)
  matrix products  40.8 us (10%)
  starting transfers between devices  20.9 us (5%)
  between operations  14.2 us (3%)
  local copies, waits for them, and re-layouts  7.54 us (2%)
    all_to_all x1, blocking collectives, shards(): lax.all_to_all(send_rows, 'expert', split_axis=0, concat_axis=0, tiled=True)  108 us
    all_to_all x1, blocking collectives, shards(): lax.all_to_all(send_scaled, 'expert', split_axis=0, concat_axis=0, tiled=...  102 us
    reduce_scatter x1, waiting for transfers between devices, shards(): lax.psum_scatter(grad_part, 'tensor', scatter_dimension=3, tiled=True)  65.7 us
    all_to_all x1, waiting for transfers between devices, shards(): lax.all_to_all(grad_sums, 'expert', split_axis=0, concat_axis=0, tiled=True)  41.3 us
    all_gather x1, blocking collectives, shards(): lax.all_gather(cotangent, 'tensor', axis=1, tiled=True)  13 us
    all_to_all x1, starting transfers between devices, shards(): lax.all_to_all(grad_sums, 'expert', split_axis=0, concat_axis=0, tiled=True)  10.7 us
  transfers between devices with their start and end apart: 5, of which 3 were waited for; matrix products, arithmetic and copies ran while one was open for 8% of the time, Pallas kernels for 0%

profile of v1, /device:TPU:2, one launch (start us, length us, event | category | flops | bytes accessed | tf_op | source)
XLA Modules:
  0.0 417.1 jit_solution(15949248251937205197)
XLA Ops:
  7.2 0.0 copy-start
  7.2 1.7 stack.2
  8.9 4.5 %all-to-all-start = ((bf16[4,32,1024]{2,1,0:T(8,128)(2,1)}), bf16[4,32,1024]{2,1,0:T(8,128)(2,1)S(1)}, u32[]{:S(2)}, u32[]{:S(2)}) async-start(bf16[4,32,1024]{2,1,0:T(8,128)(2,1)} %stack.2), calls=%async_computation | async-start | bytes 524288 | tf_op jit(solution)/shard_map/all_to_all | solution.py:10
  13.4 0.0 reduce-scatter.3.cloned.1.call-start
  13.4 0.7 bitcast_or_fusion
  14.1 0.8 copy.49
  14.8 0.1 copy.50
  14.9 0.1 reshape.85
  15.0 0.1 convert_reduce_fusion.1
  15.1 0.1 reduce_window_sum.11
  15.2 0.0 copy-start.10
  15.2 0.0 copy-start.11
  15.2 1.9 gather_fusion
  17.1 0.1 reshape.88
  17.2 0.1 copy.51
  17.3 0.0 copy-done.10
  17.3 0.0 copy-done.11
  17.3 0.1 copy.53
  17.4 0.1 copy.52
  17.5 1.0 convert_reduce_fusion
  18.5 1.5 all-to-all-done
  20.1 1.3 fusion
  21.3 0.0 copy-start.3
  21.4 108.3 %all_to_all.25 = bf16[64,1,8,4096]{3,2,1,0:T(8,128)(2,1)S(1)} all-to-all(bf16[64,1,8,4096]{3,2,1,0:T(8,128)(2,1)S(1)} %fusion), channel_id=1, replica_groups=mesh['expert'=64,'tensor'=4] {'expert'}, dimensions={0} | all-to-all | bytes 8388608 | tf_op jit(solution)/shard_map/all_to_all | solution.py:50
  129.6 0.0 copy-done.3
  129.6 0.0 copy-start.1
  129.6 2.3 fusion.18
  132.0 0.0 copy-done.1
  132.0 0.0 copy-start.5
  132.0 0.9 copy-done.5
  132.9 0.0 copy-done
  132.9 5.6 %convolution_bitcast_fusion.1 = f32[64,1,8,4096]{3,2,0,1:T(8,128)} fusion(bf16[1,384,4096]{2,1,0:T(8,128)(2,1)S(1)} %copy-done, f32[64,1,8,384]{3,2,0,1:T(8,128)S(1)} %fusion.18), kind=kOutput, calls=%fused_computation.2 | convolution fusion | flops 1611595776 | bytes 12320768 | tf_op jit(solution)/shard_map/nesh,ehd->nesd/dot_general | solution.py:56
  138.5 0.0 copy-start.9
  138.5 0.0 copy-start.7
  138.5 0.0 reduce-scatter.3.cloned.1.call-update
  138.5 0.0 reduce-scatter.5.cloned.1.call-start
  138.5 0.8 copy-done.9
  139.3 13.0 %all_gather.3 = bf16[32,4096]{1,0:T(8,128)(2,1)S(1)} all-gather(bf16[32,1024]{1,0:T(8,128)(2,1)S(1)} %copy-done.9), channel_id=1, replica_groups=mesh['expert'=64,'tensor'=4] {'tensor'}, dimensions={1}, use_global_device_ids=true | all-gather | bytes 327680 | tf_op jit(solution)/shard_map/all_gather | solution.py:35
  152.3 0.0 copy-done.7
  152.3 3.7 fusion.1
  156.0 0.0 copy-start.6
  156.0 101.9 %all_to_all.26 = bf16[64,1,8,4096]{3,2,1,0:T(8,128)(2,1)S(1)} all-to-all(bf16[64,1,8,4096]{3,2,1,0:T(8,128)(2,1)S(1)} %fusion.1), channel_id=1, replica_groups=mesh['expert'=64,'tensor'=4] {'expert'}, dimensions={0} | all-to-all | bytes 8388608 | tf_op jit(solution)/shard_map/all_to_all | solution.py:51
  258.0 0.0 copy-done.6
  258.0 0.0 copy-start.2
  258.0 0.0 copy-start.4
  258.0 2.4 fusion.43
  260.4 0.0 copy-done.2
  260.4 0.0 copy-start.8
  260.4 0.8 copy-done.8
  261.2 0.2 copy-done.4
  261.4 5.6 %convolution_bitcast_fusion = f32[64,1,8,4096]{3,2,0,1:T(8,128)} fusion(bf16[64,8,384]{2,1,0:T(8,128)(2,1)S(1)} %fusion.43, bf16[1,4096,384]{2,1,0:T(8,128)(2,1)S(1)} %copy-done.4), kind=kOutput, calls=%fused_computation.1 | convolution fusion | flops 1610612736 | bytes 11927552 | tf_op jit(solution)/shard_map/nesh,edh->nesd/dot_general | solution.py:69
  267.0 0.0 reduce-scatter.5.cloned.1.call-update
  267.0 0.0 reduce-scatter.3.cloned.1.call-done
  267.0 5.6 %all-to-all-start.2 = ((f32[64,1,8,1024]{3,2,1,0:T(8,128)}), f32[64,1,8,1024]{3,2,1,0:T(8,128)}, u32[]{:S(2)}, u32[]{:S(2)}) async-start(f32[64,1,8,1024]{3,2,1,0:T(8,128)} %bitcast.131), calls=%async_computation.3 | async-start | bytes 4194304 | tf_op jit(solution)/shard_map/all_to_all | solution.py:75
  272.7 6.5 %fusion.3 = bf16[1,384,4096]{2,1,0:T(8,128)(2,1)} fusion(bf16[64,1,8,4096]{3,2,1,0:T(8,128)(2,1)} %copy-done.2, f32[64,1,8,384]{3,2,0,1:T(8,128)} %copy-done.5), kind=kOutput, calls=%fused_computation.10 | convolution fusion | flops 1613168640 | bytes 8126464 | tf_op jit(solution)/shard_map/nesh,nesd->ehd/dot_general | solution.py:63
  279.2 65.7 %reduce-scatter.5.cloned.1.call-done = f32[64,1,8,1024]{3,2,0,1:T(8,128)} async-done(((f32[64,1,8,4096]{3,2,0,1:T(8,128)}), f32[64,1,8,1024]{3,2,0,1:T(8,128)}) %reduce-scatter.5.cloned.1.call-update) | async-done | bytes 2097168 | tf_op jit(solution)/shard_map/reduce_scatter | solution.py:72
  344.9 0.0 all-to-all-done.2
  344.9 10.7 %all-to-all-start.4 = ((f32[64,1,8,1024]{3,2,1,0:T(8,128)}), f32[64,1,8,1024]{3,2,1,0:T(8,128)}, u32[]{:S(2)}, u32[]{:S(2)}) async-start(f32[64,1,8,1024]{3,2,1,0:T(8,128)} %bitcast.132), calls=%async_computation.6 | async-start | bytes 4194304 | tf_op jit(solution)/shard_map/all_to_all | solution.py:76
  355.6 6.3 %fusion.2 = bf16[1,4096,384]{2,1,0:T(8,128)(2,1)} fusion(bf16[64,8,384]{2,1,0:T(8,128)(2,1)} %copy-done.8, bf16[64,1,8,4096]{3,2,1,0:T(8,128)(2,1)} %copy-done.1), kind=kOutput, calls=%fused_computation.9 | convolution fusion | flops 1612185600 | bytes 7733248 | tf_op jit(solution)/shard_map/nesd,nesh->edh/dot_general | solution.py:66
  361.9 3.5 fusion.48
  365.4 41.3 %all-to-all-done.4 = f32[64,1,8,1024]{3,2,1,0:T(8,128)} async-done(((f32[64,1,8,1024]{3,2,1,0:T(8,128)}), f32[64,1,8,1024]{3,2,1,0:T(8,128)}, u32[]{:S(2)}, u32[]{:S(2)}) %all-to-all-start.4) | async-done | bytes 2097184 | tf_op jit(solution)/shard_map/all_to_all | solution.py:76
  406.8 3.5 fusion.51
  (3 shorter events, 0.0 us)
Async XLA Ops:
  7.2 125.7 %copy-start = (bf16[1,384,4096]{2,1,0:T(8,128)(2,1)S(1)}, bf16[1,384,4096]{2,1,0:T(8,128)(2,1)}, u32[]{:S(2)}) copy-start(bf16[1,384,4096]{2,1,0:T(8,128)(2,1)} %param.11) | copy-start | bytes 9437188
  8.9 11.1 %all-to-all-start = ((bf16[4,32,1024]{2,1,0:T(8,128)(2,1)}), bf16[4,32,1024]{2,1,0:T(8,128)(2,1)S(1)}, u32[]{:S(2)}, u32[]{:S(2)}) async-start(bf16[4,32,1024]{2,1,0:T(8,128)(2,1)} %stack.2), calls=%async_computation | async-start | bytes 524288 | tf_op jit(solution)/shard_map/all_to_all | solution.py:10
  13.4 253.6 %reduce-scatter.3.cloned.1.call-start = ((), (), s32[]{:S(2)}) async-start(), calls=%async_computation.7 | async-start | bytes 10485760 | tf_op jit(solution)/shard_map/reduce_scatter | solution.py:71
  15.2 2.1 copy-start.10
  15.2 2.1 copy-start.11
  21.3 108.3 %copy-start.3 = (bf16[1,4096,384]{2,1,0:T(8,128)(2,1)S(1)}, bf16[1,4096,384]{2,1,0:T(8,128)(2,1)}, u32[]{:S(2)}) copy-start(bf16[1,4096,384]{2,1,0:T(8,128)(2,1)} %param.10) | copy-start | bytes 9437188
  129.6 2.3 copy-start.1
  132.0 0.9 copy-start.5
  138.5 0.8 copy-start.9
  138.5 13.8 %copy-start.7 = (f32[32,512]{1,0:T(8,128)S(1)}, f32[32,512]{1,0:T(8,128)}, u32[]{:S(2)}) copy-start(f32[32,512]{1,0:T(8,128)} %get-tuple-element.5) | copy-start | bytes 196612
  138.5 206.4 %reduce-scatter.5.cloned.1.call-start = ((), (), s32[]{:S(2)}) async-start(), calls=%async_computation.8 | async-start | bytes 10485760 | tf_op jit(solution)/shard_map/reduce_scatter | solution.py:72
  156.0 101.9 %copy-start.6 = (f32[64,1,8,384]{3,2,0,1:T(8,128)S(1)}, f32[64,1,8,384]{3,2,0,1:T(8,128)}, u32[]{:S(2)}) copy-start(f32[64,1,8,384]{3,2,0,1:T(8,128)} %copy-done.5) | copy-start | bytes 2359300
  258.0 2.5 copy-start.2
  258.0 3.4 copy-start.4
  260.4 0.8 copy-start.8
  267.0 77.8 %all-to-all-start.2 = ((f32[64,1,8,1024]{3,2,1,0:T(8,128)}), f32[64,1,8,1024]{3,2,1,0:T(8,128)}, u32[]{:S(2)}, u32[]{:S(2)}) async-start(f32[64,1,8,1024]{3,2,1,0:T(8,128)} %bitcast.131), calls=%async_computation.3 | async-start | bytes 4194304 | tf_op jit(solution)/shard_map/all_to_all | solution.py:75
  344.9 61.9 %all-to-all-start.4 = ((f32[64,1,8,1024]{3,2,1,0:T(8,128)}), f32[64,1,8,1024]{3,2,1,0:T(8,128)}, u32[]{:S(2)}, u32[]{:S(2)}) async-start(f32[64,1,8,1024]{3,2,1,0:T(8,128)} %bitcast.132), calls=%async_computation.6 | async-start | bytes 4194304 | tf_op jit(solution)/shard_map/all_to_all | solution.py:76
Sparse Core Ops, SparseCore 0:
  138.6 78.9 reduce-scatter.2
  267.1 77.7 reduce-scatter.4
